TPU v7x, 32 devices: a whole 2x2x4 slice. The times are simulated.
32 devices in a mesh: groups: 2 (over x), seq: 16 (over z, y, core).
Axes of the slice: x: 2, y: 2, z: 4, core: 2. Of those that a mesh axis runs over, the one named last changes fastest.
Arguments:
- features: bfloat16 [16384, 1024], P(('groups', 'seq')), parts along dimension 0, may hold values from -6 to 6
- attention_gain: float32 [1024], replicated, may hold values from 0.1 to 1.9
- qkv_weight: bfloat16 [1024, 3072], replicated, may hold values from -0.1875 to 0.1875
- out_weight: bfloat16 [1024, 1024], replicated, may hold values from -0.1875 to 0.1875
- mlp_gain: float32 [1024], replicated, may hold values from 0.1 to 1.9
- up_weight: bfloat16 [1024, 2048], P(None, 'seq'), may hold values from -0.1875 to 0.1875
- down_weight: bfloat16 [2048, 1024], P('seq'), may hold values from -0.125 to 0.125
- block_columns: int32 [128, 8], P('groups'), parts along dimension 0, may hold values from 0 to 63, as said below
- block_counts: int32 [128], P('groups'), parts along dimension 0, may hold values from 1 to 8, as said below
- global_nodes: int32 [1024], P('groups'), parts along dimension 0, may hold values from 0 to 8191, as said below
Outputs:
- layer_out: bfloat16 [16384, 1024], P(('groups', 'seq')), parts along dimension 0
There are 2 independent parts, one for each index of `groups`. A program takes and returns all parts, laid end to end along the dimension named above; an argument that names none is the same for every part. Nothing has to cross between parts.
Inputs may be any that keep to these rules, and one draw needn't show every extreme that they name: In every row of block_columns the 8 entries are distinct block numbers. `block_counts`: some row block uses all 8 listed column blocks. `global_nodes`: the 512 global nodes are distinct.
All inputs are finite; a program needn't handle non-finite values.
Results may differ from a plain program's by a relative error of at most 0.005.
Values may be sent and summed in bfloat16 or wider, within the bound.
A program may use at most 128 MiB of HBM per device.

v0:
```python
import jax
import jax.numpy as jnp
from jax import lax
from jax.sharding import PartitionSpec as P

HEADS = 16
BLOCK = 128


EPS = 1e-05


def layer_norm(values, gain):
    values = values.astype(jnp.float32)
    average = jnp.mean(values, axis=-1, keepdims=True)
    centered = values - average
    variance = jnp.mean(centered * centered, axis=-1, keepdims=True)
    return centered * lax.rsqrt(variance + EPS) * gain


def attend_group(queries, memory_blocks, memory_global, global_block, columns, counts):
    groups, block_rows, head_dim = queries.shape
    slot_count = columns.shape[1]
    in_list = jnp.arange(slot_count, dtype=jnp.int32)[None, :] < counts[:, None]
    picked = memory_blocks[columns].reshape(groups, slot_count * block_rows, 2 * head_dim)
    score_scale = head_dim ** (-0.5)
    local_scores = (
        jnp.einsum(
            "gqd,gkd->gqk", queries, picked[:, :, :head_dim], preferred_element_type=jnp.float32
        )
        * score_scale
    )
    key_mask = jnp.repeat(in_list, block_rows, axis=1)[:, None, :]
    local_weights = jnp.where(key_mask, jnp.exp(local_scores), 0.0)
    duplicate = jnp.any(
        in_list[:, :, None] & (columns[:, :, None] == global_block[None, None, :]), axis=1
    )
    global_scores = (
        jnp.einsum(
            "gqd,nd->gqn", queries, memory_global[:, :head_dim], preferred_element_type=jnp.float32
        )
        * score_scale
    )
    global_weights = jnp.where(duplicate[:, None, :], 0.0, jnp.exp(global_scores))
    totals = jnp.sum(local_weights, axis=-1, keepdims=True) + jnp.sum(
        global_weights, axis=-1, keepdims=True
    )
    local_probs = (local_weights / totals).astype(jnp.bfloat16)
    global_probs = (global_weights / totals).astype(jnp.bfloat16)
    result = jnp.einsum(
        "gqk,gkd->gqd", local_probs, picked[:, :, head_dim:], preferred_element_type=jnp.float32
    )
    result = result + jnp.einsum(
        "gqn,nd->gqd", global_probs, memory_global[:, head_dim:], preferred_element_type=jnp.float32
    )
    return result.astype(jnp.bfloat16)


def on_device(
    features,
    attention_gain,
    qkv_weight,
    out_weight,
    mlp_gain,
    up_weight,
    down_weight,
    block_columns,
    block_counts,
    global_nodes,
):
    node_count, model_width = features.shape
    devices = lax.axis_size("seq")
    head_dim = model_width // HEADS
    repeat = devices // HEADS
    sub_rows = node_count // repeat
    lane_pack = max(1, 128 // head_dim)
    position = lax.axis_index("seq")
    sub_index = position % repeat
    normed = layer_norm(features, attention_gain).astype(jnp.bfloat16)
    packed = jnp.dot(normed, qkv_weight, preferred_element_type=jnp.float32).astype(jnp.bfloat16)
    query_part = (
        packed[:, :model_width].reshape(repeat, sub_rows, HEADS, head_dim).transpose(2, 0, 1, 3)
    )
    query_send = query_part.reshape(HEADS * repeat * sub_rows // lane_pack, lane_pack * head_dim)
    query_recv = lax.all_to_all(query_send, "seq", split_axis=0, concat_axis=0, tiled=True)
    queries = query_recv.reshape(devices * sub_rows, head_dim)
    key_part = packed[:, model_width : 2 * model_width].reshape(node_count, HEADS, head_dim)
    value_part = packed[:, 2 * model_width :].reshape(node_count, HEADS, head_dim)
    memory_local = jnp.concatenate((key_part, value_part), axis=2).transpose(1, 0, 2)
    memory_send = jnp.broadcast_to(memory_local[:, None], (HEADS, repeat, node_count, 2 * head_dim))
    memory_send = memory_send.reshape(HEADS * repeat * node_count, 2 * head_dim)
    head_memory = lax.all_to_all(memory_send, "seq", split_axis=0, concat_axis=0, tiled=True)
    total_blocks = devices * node_count // BLOCK
    memory_blocks = head_memory.reshape(total_blocks, BLOCK, 2 * head_dim)
    memory_global = head_memory[global_nodes]
    global_block = global_nodes // BLOCK
    local_blocks = devices * sub_rows // BLOCK
    sub_blocks = sub_rows // BLOCK
    block_order = jnp.arange(local_blocks, dtype=jnp.int32)
    block_ids = (
        block_order // sub_blocks * (node_count // BLOCK)
        + sub_index * sub_blocks
        + block_order % sub_blocks
    )
    turn_ids = block_ids.reshape(local_blocks // 4, 4)
    query_turns = queries.reshape(local_blocks // 4, 4, BLOCK, head_dim)

    def one_turn(turn_item):
        chosen_ids, query_group = turn_item
        return attend_group(
            query_group,
            memory_blocks,
            memory_global,
            global_block,
            block_columns[chosen_ids],
            block_counts[chosen_ids],
        )

    attended = lax.map(one_turn, (turn_ids, query_turns))
    attended_send = attended.reshape(devices * sub_rows // lane_pack, lane_pack * head_dim)
    returned = lax.all_to_all(attended_send, "seq", split_axis=0, concat_axis=0, tiled=True)
    attended_rows = (
        returned.reshape(HEADS, repeat, sub_rows, head_dim)
        .transpose(1, 2, 0, 3)
        .reshape(node_count, model_width)
    )
    mixed_rows = features.astype(jnp.float32) + jnp.dot(
        attended_rows, out_weight, preferred_element_type=jnp.float32
    )
    normed_mlp = layer_norm(mixed_rows, mlp_gain).astype(jnp.bfloat16)
    hidden = jax.nn.gelu(
        jnp.dot(
            normed_mlp,
            lax.all_gather(up_weight, "seq", axis=1, tiled=True),
            preferred_element_type=jnp.float32,
        ),
        approximate=True,
    ).astype(jnp.bfloat16)
    reduced = jnp.dot(
        hidden,
        lax.all_gather(down_weight, "seq", axis=0, tiled=True),
        preferred_element_type=jnp.float32,
    )
    return (mixed_rows + reduced).astype(jnp.bfloat16)


def solution(mesh):
    in_specs = (
        P(("groups", "seq"), None),
        P(),
        P(),
        P(),
        P(),
        P(None, "seq"),
        P("seq", None),
        P("groups", None),
        P("groups"),
        P("groups"),
    )
    out_specs = P(("groups", "seq"), None)
    return jax.shard_map(
        on_device, mesh=mesh, in_specs=in_specs, out_specs=out_specs, check_vma=False
    )
```

profile of v0, /device:TPU:0, one launch (start us, length us, event | category | flops | bytes accessed | tf_op | source)
XLA Modules:
  0.0 364.0 jit_solution(10347358104408994524)
XLA Ops:
  8.7 1.6 fusion.36
  10.4 6.7 %convolution_convert_fusion = bf16[512,3072]{1,0:T(8,128)(2,1)S(1)} fusion(bf16[1024,3072]{1,0:T(8,128)(2,1)} %param.14, bf16[512,1024]{1,0:T(8,128)(2,1)S(1)} %copy-done.2, f32[1024]{0:T(1024)S(1)} %copy-done.7, f32[512]{0:T(512)S(1)} %add_rsqrt_fusion.1, f32[512]{0:T(512)S(1)} %broadcast_multiply_fusion.1), kind=kOutput, calls=%fused_computation.45 | convolution fusion | flops 3225419776 | bytes 10493952 | tf_op jit(solution)/shard_map/dot_general | solution.py:80
  17.0 1.7 fusion.72
  20.3 1.8 copy.43
  22.1 3.9 %all_to_all.18 = bf16[16,256,128]{2,1,0:T(8,128)(2,1)} reshape(bf16[16,1,512,64]{3,2,0,1:T(8,128)(2,1)} %copy.43) | data formatting | bytes 2097152 | tf_op jit(solution)/shard_map/all_to_all | solution.py:85
  26.0 7.4 %all-to-all-start = ((bf16[16,256,128]{2,1,0:T(8,128)(2,1)}), bf16[16,256,128]{2,1,0:T(8,128)(2,1)S(1)}, u32[]{:S(2)}, u32[]{:S(2)}) async-start(bf16[16,256,128]{2,1,0:T(8,128)(2,1)} %all_to_all.18), calls=%async_computation | async-start | bytes 2097152 | tf_op jit(solution)/shard_map/all_to_all | solution.py:85
  33.4 2.3 copy.44
  35.7 2.3 copy.45
  38.0 3.1 maximum_bitcast_fusion
  41.1 25.0 %all-to-all-done = bf16[16,256,128]{2,1,0:T(8,128)(2,1)S(1)} async-done(((bf16[16,256,128]{2,1,0:T(8,128)(2,1)}), bf16[16,256,128]{2,1,0:T(8,128)(2,1)S(1)}, u32[]{:S(2)}, u32[]{:S(2)}) %all-to-all-start) | async-done | bytes 1048608 | tf_op jit(solution)/shard_map/all_to_all | solution.py:85
  66.1 13.9 %all-to-all-start.1 = ((bf16[16,512,128]{1,2,0:T(8,128)(2,1)}), bf16[16,512,128]{1,2,0:T(8,128)(2,1)}, u32[]{:S(2)}, u32[]{:S(2)}) async-start(bf16[16,512,128]{1,2,0:T(8,128)(2,1)} %maximum_bitcast_fusion), calls=%async_computation.1 | async-start | bytes 4194304 | tf_op jit(solution)/shard_map/all_to_all | solution.py:92
  80.9 1.8 reshape_reshape.3
  82.7 2.7 copy.48
  85.4 44.1 %all-to-all-done.1 = bf16[16,512,128]{1,2,0:T(8,128)(2,1)} async-done(((bf16[16,512,128]{1,2,0:T(8,128)(2,1)}), bf16[16,512,128]{1,2,0:T(8,128)(2,1)}, u32[]{:S(2)}, u32[]{:S(2)}) %all-to-all-start.1) | async-done | bytes 2097184 | tf_op jit(solution)/shard_map/all_to_all | solution.py:92
  129.6 3.9 %copy.46 = bf16[16,512,128]{2,1,0:T(8,128)(2,1)} copy(bf16[16,512,128]{1,2,0:T(8,128)(2,1)} %all-to-all-done.1) | data formatting | bytes 4194304 | tf_op jit(solution)/shard_map/all_to_all | solution.py:92
  133.5 2.9 gather_fusion.3
  136.5 142.7 %while.10 = (s32[]{:T(128)}, bf16[16,4,128,64]{2,3,1,0:T(8,128)(2,1)}, s32[16,4]{1,0:T(8,128)S(1)}, s32[64]{0:T(128)S(1)}, bf16[16,4,128,64]{2,3,1,0:T(8,128)(2,...) while((s32[]{:T(128)}, ...), condition=%wide.region_6.7_spmd, body=%wide.region_2.6_spmd.sunk | while | flops 206421648 | bytes 11127753 | solution.py:119
  137.2 2.3 gather_fusion.1
  146.2 2.3 gather_fusion.1
  149.3 1.5 fusion.89
  155.1 2.3 gather_fusion.1
  158.2 1.5 fusion.89
  164.0 2.3 gather_fusion.1
  167.2 1.5 fusion.89
  172.9 2.3 gather_fusion.1
  176.1 1.5 fusion.89
  181.8 2.3 gather_fusion.1
  185.0 1.5 fusion.89
  190.8 2.3 gather_fusion.1
  193.9 1.5 fusion.89
  199.7 2.3 gather_fusion.1
  202.8 1.5 fusion.89
  208.6 2.3 gather_fusion.1
  211.8 1.5 fusion.89
  217.5 2.3 gather_fusion.1
  226.4 2.3 gather_fusion.1
  235.4 2.3 gather_fusion.1
  244.3 2.3 gather_fusion.1
  253.2 2.3 gather_fusion.1
  262.1 2.3 gather_fusion.1
  271.0 2.3 gather_fusion.1
  279.3 2.7 copy.51
  282.0 3.0 all_to_all.22
  285.0 50.9 %all_to_all.27 = bf16[16,256,128]{2,1,0:T(8,128)(2,1)} all-to-all(bf16[16,256,128]{2,1,0:T(8,128)(2,1)S(1)} %all_to_all.22), channel_id=1, replica_groups=mesh['groups'=2,'seq'=16] {'seq'}, dimensions={0} | all-to-all | bytes 2097152 | tf_op jit(solution)/shard_map/all_to_all | solution.py:121
  335.9 3.8 %reshape.146 = bf16[16,1,512,64]{3,2,0,1:T(8,128)(2,1)} reshape(bf16[16,256,128]{2,1,0:T(8,128)(2,1)} %all_to_all.27) | data formatting | bytes 2097152 | tf_op jit(solution)/shard_map/reshape | solution.py:123
  339.8 2.8 copy.52
  342.5 2.6 fusion.73
  346.9 10.3 %add_convert_fusion = bf16[512,1024]{1,0:T(8,128)(2,1)} fusion(f32[512,1024]{1,0:T(8,128)} %copy-done.4, bf16[2048,1024]{1,0:T(8,128)(2,1)} %all-gather.5.cloned.1.call-done, bf16[1024,2048]{1,0:T(8,128)(2,1)} %all-gather.3.cloned.1.call-done, f32[1024]{0:T(1024)S(1)} %copy-done.8, f32[512]{0:T(512)S(1)} %add_rsqrt_fusion, f32[512]{0:T(512)S(1)} %broadcast_multiply_fusion), kind=kOutput, calls=%fused_computation.64 | convolution fusion | flops 4307550208 | bytes 11542528 | tf_op jit(solution)/shard_map/dot_general | solution.py:139
  (285 shorter events, 98.9 us)
Async XLA Ops:
  6.5 336.0 %copy-start = (bf16[1024,1024]{1,0:T(8,128)(2,1)S(1)}, bf16[1024,1024]{1,0:T(8,128)(2,1)}, u32[]{:S(2)}) copy-start(bf16[1024,1024]{1,0:T(8,128)(2,1)} %param.15) | copy-start | bytes 6291460
  6.5 3.8 %copy-start.2 = (bf16[512,1024]{1,0:T(8,128)(2,1)S(1)}, bf16[512,1024]{1,0:T(8,128)(2,1)}, u32[]{:S(2)}) copy-start(bf16[512,1024]{1,0:T(8,128)(2,1)} %param.12) | copy-start | bytes 3145732
  6.5 3.8 %copy-start.7 = (f32[1024]{0:T(1024)S(1)}, f32[1024]{0:T(1024)}, u32[]{:S(2)}) copy-start(f32[1024]{0:T(1024)} %param.13) | copy-start | bytes 12292
  6.5 340.3 %all-gather.3.cloned.1.call-start = ((), (), s32[]{:S(2)}) async-start(), calls=%async_computation.3 | async-start | bytes 4456448 | tf_op jit(solution)/shard_map/all_gather | solution.py:134
  26.0 40.1 %all-to-all-start = ((bf16[16,256,128]{2,1,0:T(8,128)(2,1)}), bf16[16,256,128]{2,1,0:T(8,128)(2,1)S(1)}, u32[]{:S(2)}, u32[]{:S(2)}) async-start(bf16[16,256,128]{2,1,0:T(8,128)(2,1)} %all_to_all.18), calls=%async_computation | async-start | bytes 2097152 | tf_op jit(solution)/shard_map/all_to_all | solution.py:85
  41.1 39.7 %copy-start.5 = (s32[64,8]{0,1:T(8,128)S(1)}, s32[64,8]{0,1:T(8,128)}, u32[]{:S(2)}) copy-start(s32[64,8]{0,1:T(8,128)} %param.19) | copy-start | bytes 6148
  41.1 39.8 %copy-start.6 = (s32[512]{0:T(512)S(1)}, s32[512]{0:T(512)}, u32[]{:S(2)}) copy-start(s32[512]{0:T(512)} %param.21) | copy-start | bytes 6148
  66.1 63.5 %all-to-all-start.1 = ((bf16[16,512,128]{1,2,0:T(8,128)(2,1)}), bf16[16,512,128]{1,2,0:T(8,128)(2,1)}, u32[]{:S(2)}, u32[]{:S(2)}) async-start(bf16[16,512,128]{1,2,0:T(8,128)(2,1)} %maximum_bitcast_fusion), calls=%async_computation.1 | async-start | bytes 4194304 | tf_op jit(solution)/shard_map/all_to_all | solution.py:92
  80.0 266.9 %all-gather.5.cloned.1.call-start = ((), (), s32[]{:S(2)}) async-start(), calls=%async_computation.4 | async-start | bytes 4456448 | tf_op jit(solution)/shard_map/all_gather | solution.py:141
  85.4 51.1 %copy-start.1 = (s32[64]{0:T(128)S(1)}, s32[64]{0:T(128)}, u32[]{:S(2)}) copy-start(s32[64]{0:T(128)} %param.20) | copy-start | bytes 772
  339.8 2.8 copy-start.3
  345.1 1.4 copy-start.4
  345.1 1.8 copy-start.8
Sparse Core Ops, SparseCore 0:
  9.5 69.5 all-gather.2
  83.0 72.9 all-gather.4
where the time goes:
time: 367 us; the launch traced here: 364 us
  matrix products  99.1 us (27%)
  local copies, waits for them, and re-layouts  98.1 us (27%)
  waiting for transfers between devices  70.6 us (19%)
  blocking collectives  50.9 us (14%)
  starting transfers between devices  21.3 us (6%)
  between operations  13.6 us (4%)
  other arithmetic  9.99 us (3%)
    all_to_all x1, blocking collectives, on_device(): lax.all_to_all(attended_send, 'seq', split_axis=0, concat_axis=0, tiled=T...  50.9 us
    all_to_all x1, waiting for transfers between devices, on_device(): lax.all_to_all(memory_send, 'seq', split_axis=0, concat_axis=0, tiled=True)  44.1 us
    gather x16, local copies, waits for them, and re-layouts, attend_group(): memory_blocks[columns]  37.4 us
    all_to_all x1, waiting for transfers between devices, on_device(): lax.all_to_all(query_send, 'seq', split_axis=0, concat_axis=0, tiled=True)  25 us
    dot_general x16, matrix products, attend_group(): jnp.einsum('gqd,gkd->gqk', queries, picked[:, :, :head_dim], preferred_el...  24.6 us
    dot_general x16, matrix products, attend_group(): jnp.einsum('gqd,nd->gqn', queries, memory_global[:, :head_dim], preferred...  20.6 us
    dot_general x16, matrix products, attend_group(): jnp.einsum('gqk,gkd->gqd', local_probs, picked[:, :, head_dim:], preferre...  18.1 us
    dot_general x16, matrix products, attend_group(): jnp.einsum('gqn,nd->gqd', global_probs, memory_global[:, head_dim:], pref...  16.2 us
  transfers between devices with their start and end apart: 4, of which 2 were waited for; matrix products, arithmetic and copies ran while one was open for 52% of the time, Pallas kernels for 0%

commit v1 on v0

v1 whole, which is shorter than its diff:
```python
import functools

import jax
import jax.numpy as jnp
from jax import lax
from jax.experimental import pallas as pl
from jax.experimental.pallas import tpu as pltpu
from jax.sharding import PartitionSpec as P

HEADS = 16
BLOCK = 128
EPS = 1e-05
MASKED = -1e30


def layer_norm(values, gain):
    values = values.astype(jnp.float32)
    average = jnp.mean(values, axis=-1, keepdims=True)
    centered = values - average
    variance = jnp.mean(centered * centered, axis=-1, keepdims=True)
    return centered * lax.rsqrt(variance + EPS) * gain


def swap_halves(left, right):
    low = lax.broadcasted_iota(jnp.int32, left.shape, 1) < 64
    return (
        jnp.where(low, left, pltpu.roll(right, 64, 1)),
        jnp.where(low, pltpu.roll(left, 64, 1), right),
    )


def attention_kernel(
    n,
    repeat,
    x_ref,
    gain_ref,
    w_ref,
    bias_ref,
    gidx_ref,
    cols_ref,
    out_ref,
    normed,
    kv_out,
    memory,
    q_out,
    q_in,
    o_out,
    o_in,
    global_sum,
    global_kv,
    kv_send,
    kv_recv,
    q_send,
    q_recv,
    o_send,
    o_recv,
):
    rows, width = x_ref.shape
    sub_rows = rows // repeat
    half = sub_rows // 2
    blocks = rows // BLOCK
    slots = cols_ref.shape[1]
    me = lax.axis_index("seq")
    my_head, my_sub = me // repeat, me % repeat
    f32, bf16 = jnp.float32, jnp.bfloat16

    barrier = pltpu.get_barrier_semaphore()

    def greet(step, carry):
        peer = (me + step) % n
        pl.semaphore_signal(
            barrier, inc=1, device_id={"seq": peer}, device_id_type=pl.DeviceIdType.MESH
        )
        return carry

    lax.fori_loop(1, n, greet, 0)

    def kv_copy(head, owner, source):
        return pltpu.make_async_remote_copy(
            src_ref=kv_out.at[head],
            dst_ref=memory.at[pl.ds(source * blocks, blocks)],
            send_sem=kv_send.at[owner],
            recv_sem=kv_recv.at[source],
            device_id={"seq": owner},
            device_id_type=pl.DeviceIdType.MESH,
        )

    def q_copy(owner, source):
        return pltpu.make_async_remote_copy(
            src_ref=q_out.at[owner],
            dst_ref=q_in.at[source],
            send_sem=q_send.at[owner],
            recv_sem=q_recv.at[source],
            device_id={"seq": owner},
            device_id_type=pl.DeviceIdType.MESH,
        )

    def o_copy(home, worker):
        return pltpu.make_async_remote_copy(
            src_ref=o_out.at[home],
            dst_ref=o_in.at[worker],
            send_sem=o_send.at[home],
            recv_sem=o_recv.at[worker],
            device_id={"seq": home},
            device_id_type=pl.DeviceIdType.MESH,
        )

    def norm_rows(i, carry):
        at = pl.ds(pl.multiple_of(i * BLOCK, BLOCK), BLOCK)
        normed[at, :] = layer_norm(x_ref[at, :], gain_ref[...]).astype(bf16)
        return carry

    lax.fori_loop(0, rows // BLOCK, norm_rows, 0)
    pl.semaphore_wait(barrier, n - 1)

    def quad_of(i):
        return (me // (4 * repeat) + 1 + i) % (HEADS // 4)

    def project(first, quad):
        columns = pl.ds(pl.multiple_of(first * width + quad * 256, 256), 256)
        return jnp.dot(normed[...], w_ref[:, columns], preferred_element_type=f32)

    def kv_quad(i, carry):
        quad = quad_of(i)
        keys = project(1, quad)
        values = project(2, quad)
        for pair in range(2):
            at = slice(pair * 128, pair * 128 + 128)
            first, second = swap_halves(keys[:, at], values[:, at])
            kv_out[quad * 4 + 2 * pair] = first.astype(bf16).reshape(blocks, BLOCK, 128)
            kv_out[quad * 4 + 2 * pair + 1] = second.astype(bf16).reshape(blocks, BLOCK, 128)
        for inner in range(4):
            head = quad * 4 + inner
            for sub in range(repeat):
                owner = head * repeat + sub

                @pl.when(owner != me)
                def _():
                    kv_copy(head, owner, me).start()

        return carry

    lax.fori_loop(0, HEADS // 4, kv_quad, 0)

    def q_quad(i, carry):
        quad = quad_of(i)
        queries = project(0, quad) * 0.125
        for pair in range(2):
            both = queries[:, pair * 128 : pair * 128 + 128]
            for sub in range(repeat):
                top = both[sub * sub_rows : sub * sub_rows + half]
                bottom = both[sub * sub_rows + half : (sub + 1) * sub_rows]
                first, second = swap_halves(top, bottom)
                head = quad * 4 + 2 * pair
                q_out[head * repeat + sub] = first.astype(bf16)
                q_out[(head + 1) * repeat + sub] = second.astype(bf16)
        for inner in range(4):
            for sub in range(repeat):
                owner = (quad * 4 + inner) * repeat + sub

                @pl.when(owner != me)
                def _():
                    q_copy(owner, me).start()

        return carry

    lax.fori_loop(0, HEADS // 4, q_quad, 0)

    memory[pl.ds(me * blocks, blocks)] = kv_out[my_head]
    q_in[me] = q_out[me]

    global_sum[...] = jnp.zeros_like(global_sum)

    def arrive(step, carry):
        source = (me + n - step) % n

        @pl.when(source != me)
        def _():
            kv_copy(my_head, me, source).wait_recv()

        offset = gidx_ref[...] - source * rows
        spot = lax.broadcasted_iota(jnp.int32, (offset.shape[0], rows), 1)
        chosen = jnp.where(spot == offset, 1.0, 0.0).astype(bf16)
        chunk = memory[pl.ds(source * blocks, blocks)].reshape(rows, 128)
        global_sum[...] += jnp.dot(chosen, chunk, preferred_element_type=f32)
        return carry

    lax.fori_loop(0, n, arrive, 0)
    global_kv[...] = global_sum[...].astype(bf16)

    def serve(step, carry):
        source = (me + n - step) % n

        @pl.when(source != me)
        def _():
            q_copy(me, source).wait_recv()

        packed = q_in[source].astype(f32)
        low = lax.broadcasted_iota(jnp.int32, packed.shape, 1) < 64
        top = jnp.where(low, packed, 0.0).astype(bf16)
        bottom = jnp.where(low, pltpu.roll(packed, 64, 1), 0.0).astype(bf16)
        queries = jnp.concatenate((top, bottom), axis=0)
        results = []
        for r in range(sub_rows // BLOCK):
            block = source * (rows // BLOCK) + my_sub * (sub_rows // BLOCK) + r
            picked = [memory[cols_ref[block, j]] for j in range(slots)]
            kv = jnp.concatenate(picked + [global_kv[...]], axis=0)
            scores = lax.dot_general(
                queries[r * BLOCK : (r + 1) * BLOCK],
                kv,
                (((1,), (1,)), ((), ())),
                preferred_element_type=f32,
            )
            weights = jnp.exp(scores + bias_ref[pl.ds(block, 1), :])
            totals = jnp.sum(weights, axis=1, keepdims=True)
            scale = jnp.where(totals > 1.0, 2.0**-10, 1.0)
            probs = (weights * (1.0 / (totals * scale))).astype(bf16)
            results.append(jnp.dot(probs, kv, preferred_element_type=f32) * scale)
        result = jnp.concatenate(results, axis=0)
        top, bottom = result[:half], result[half:]
        o_out[source] = jnp.where(low, pltpu.roll(top, 64, 1), bottom).astype(bf16)

        @pl.when(source != me)
        def _():
            o_copy(source, me).start()

        return carry

    lax.fori_loop(0, n, serve, 0)
    o_in[me] = o_out[me]

    def settle(step, carry):
        peer = (me + step) % n
        o_copy(me, peer).wait_recv()
        kv_copy(peer // repeat, peer, me).wait_send()
        q_copy(peer, me).wait_send()
        o_copy(peer, me).wait_send()
        return carry

    lax.fori_loop(1, n, settle, 0)

    for pair in range(HEADS // 2):
        for sub in range(repeat):
            first = o_in[2 * pair * repeat + sub].astype(f32)
            second = o_in[(2 * pair + 1) * repeat + sub].astype(f32)
            top, bottom = swap_halves(first, second)
            at = slice(pair * 128, pair * 128 + 128)
            out_ref[sub * sub_rows : sub * sub_rows + half, at] = top.astype(bf16)
            out_ref[sub * sub_rows + half : (sub + 1) * sub_rows, at] = bottom.astype(bf16)


def attend(features, gain, weight, bias, global_nodes, columns):
    n = lax.axis_size("seq")
    repeat = n // HEADS
    rows, width = features.shape
    half = rows // repeat // 2
    globals_count = global_nodes.shape[0]
    bf16 = jnp.bfloat16
    vmem = pl.BlockSpec(memory_space=pltpu.VMEM)
    flops = 2 * rows * width * 3 * width + 4 * rows * HEADS * 64 * bias.shape[1]
    return pl.pallas_call(
        functools.partial(attention_kernel, n, repeat),
        out_shape=jax.ShapeDtypeStruct((rows, width), bf16),
        in_specs=[vmem] * 5 + [pl.BlockSpec(memory_space=pltpu.SMEM)],
        out_specs=vmem,
        scratch_shapes=[
            pltpu.VMEM((rows, width), bf16),
            pltpu.VMEM((HEADS, rows // BLOCK, BLOCK, 128), bf16),
            pltpu.VMEM((n * rows // BLOCK, BLOCK, 128), bf16),
            pltpu.VMEM((n, half, 128), bf16),
            pltpu.VMEM((n, half, 128), bf16),
            pltpu.VMEM((n, half, 128), bf16),
            pltpu.VMEM((n, half, 128), bf16),
            pltpu.VMEM((globals_count, 128), jnp.float32),
            pltpu.VMEM((globals_count, 128), bf16),
        ]
        + [pltpu.SemaphoreType.DMA((n,))] * 6,
        compiler_params=pltpu.CompilerParams(
            collective_id=0, has_side_effects=True, vmem_limit_bytes=48 * 2**20
        ),
        cost_estimate=pl.CostEstimate(
            flops=flops * 16, bytes_accessed=2**24, transcendentals=rows * HEADS * bias.shape[1]
        ),
        name="attend",
    )(features, gain[None, :], weight, bias, global_nodes[:, None], columns)


def on_device(
    features,
    attention_gain,
    qkv_weight,
    out_weight,
    mlp_gain,
    up_weight,
    down_weight,
    block_columns,
    block_counts,
    global_nodes,
):
    slots = block_columns.shape[1]
    in_list = jnp.arange(slots, dtype=jnp.int32)[None, :] < block_counts[:, None]
    global_block = global_nodes // BLOCK
    duplicate = jnp.any(
        in_list[:, :, None] & (block_columns[:, :, None] == global_block[None, None, :]), axis=1
    )
    bias = jnp.concatenate(
        (
            jnp.repeat(jnp.where(in_list, 0.0, MASKED), BLOCK, axis=1),
            jnp.where(duplicate, MASKED, 0.0),
        ),
        axis=1,
    ).astype(jnp.float32)
    attended_rows = attend(
        features, attention_gain, qkv_weight, bias, global_nodes, block_columns
    )
    mixed_rows = features.astype(jnp.float32) + jnp.dot(
        attended_rows, out_weight, preferred_element_type=jnp.float32
    )
    normed_mlp = layer_norm(mixed_rows, mlp_gain).astype(jnp.bfloat16)
    hidden = jax.nn.gelu(
        jnp.dot(
            normed_mlp,
            lax.all_gather(up_weight, "seq", axis=1, tiled=True),
            preferred_element_type=jnp.float32,
        ),
        approximate=True,
    ).astype(jnp.bfloat16)
    reduced = jnp.dot(
        hidden,
        lax.all_gather(down_weight, "seq", axis=0, tiled=True),
        preferred_element_type=jnp.float32,
    )
    return (mixed_rows + reduced).astype(jnp.bfloat16)


def solution(mesh):
    in_specs = (
        P(("groups", "seq"), None),
        P(),
        P(),
        P(),
        P(),
        P(None, "seq"),
        P("seq", None),
        P("groups", None),
        P("groups"),
        P("groups"),
    )
    out_specs = P(("groups", "seq"), None)
    return jax.shard_map(
        on_device, mesh=mesh, in_specs=in_specs, out_specs=out_specs, check_vma=False
    )
```

time: 367 us -> 196 us (0.53)
  Pallas kernels: 0 us -> 141 us
  local copies, waits for them, and re-layouts: 98.1 us -> 3.83 us
  matrix products: 99.1 us -> 11.6 us
  blocking collectives: 50.9 us -> 0 us
  waiting for transfers between devices: 70.6 us -> 20.9 us
  starting transfers between devices: 21.3 us -> 0.04 us
  other arithmetic: 9.99 us -> 4.65 us
    pallas_call x0 -> x1, Pallas kernels: none -> 141 us  [attend(): pl.pallas_call(functools.partial(attention_kernel, n, repeat), out_shape=...]
    dot_general x65 -> x0, matrix products: 86.2 us -> none  [the longest x16 24.6 us: attend_group(): jnp.einsum('gqd,gkd->gqk', queries, picked[:, :, :head_dim], preferred_el...]
    all_to_all x2 -> x0, waiting for transfers between devices: 69.2 us -> none  [the longest x1 44.1 us: on_device(): lax.all_to_all(memory_send, 'seq', split_axis=0, concat_axis=0, tiled=True)]
    gather x49 -> x0, local copies, waits for them, and re-layouts: 59.5 us -> none  [the longest x16 37.4 us: attend_group(): memory_blocks[columns]]
    all_to_all x1 -> x0, blocking collectives: 50.9 us -> none  [on_device(): lax.all_to_all(attended_send, 'seq', split_axis=0, concat_axis=0, tiled=T...]
    all_to_all x2 -> x0, starting transfers between devices: 21.3 us -> none  [the longest x1 13.9 us: on_device(): lax.all_to_all(memory_send, 'seq', split_axis=0, concat_axis=0, tiled=True)]
    all_gather x1, waiting for transfers between devices: 0.02 us -> 19.5 us  [on_device(): lax.all_gather(down_weight, 'seq', axis=0, tiled=True)]
    all_to_all x3 -> x0, local copies, waits for them, and re-layouts: 10.8 us -> none  [the longest x1 3.91 us: on_device(): lax.all_to_all(query_send, 'seq', split_axis=0, concat_axis=0, tiled=True)]
  transfers between devices with their start and end apart: 4 -> 2, of which waited for: 2 -> 1; matrix products, arithmetic and copies ran while one was open for 52% -> 4% of each run, Pallas kernels for 0% -> 72%
where the time goes in v1:
time: 196 us
  Pallas kernels  141 us (72%)
  waiting for transfers between devices  20.9 us (11%)
  between operations  13.5 us (7%)
  matrix products  11.6 us (6%)
  other arithmetic  4.65 us (2%)
  local copies, waits for them, and re-layouts  3.83 us (2%)
    pallas_call x1, Pallas kernels, attend(): pl.pallas_call(functools.partial(attention_kernel, n, repeat), out_shape=...  141 us
    all_gather x1, waiting for transfers between devices, on_device(): lax.all_gather(down_weight, 'seq', axis=0, tiled=True)  19.5 us
    dot_general x1, matrix products, on_device(): jnp.dot(hidden, lax.all_gather(down_weight, 'seq', axis=0, tiled=True), p...  10.3 us
  transfers between devices with their start and end apart: 2, of which 1 were waited for; matrix products, arithmetic and copies ran while one was open for 4% of the time, Pallas kernels for 72%

profile of v1, /device:TPU:0, one launch (start us, length us, event | category | flops | bytes accessed | tf_op | source)
XLA Modules:
  0.0 195.8 jit_solution(7134563782231881971)
XLA Ops:
  6.5 0.0 copy-start
  6.5 0.0 copy-start.1
  6.5 0.0 copy-start.2
  6.5 0.0 all-gather.3.cloned.1.call-start
  6.5 0.7 all-gather.3.cloned.1.call-update
  7.3 0.0 all-gather.5.cloned.1.call-start
  7.3 0.7 all-gather.5.cloned.1.call-update
  8.0 0.7 iota_compare_fusion
  8.8 0.7 broadcast_select_fusion.1
  9.5 0.7 add_select_fusion
  10.2 0.8 copy.16.cols_ref
  10.9 0.4 and_reduce_fusion
  11.4 0.7 broadcast_select_fusion
  12.0 0.1 broadcast_in_dim.36
  12.2 0.8 copy.21
  12.9 0.8 copy.17.gidx_ref
  13.8 1.0 pad_maximum_fusion.bias_ref
  14.8 0.0 copy-done.1
  14.8 0.0 copy-done.2
  14.8 141.3 %attend.1 = bf16[512,1024]{1,0:T(8,128)(2,1)S(1)} custom-call(bf16[512,1024]{1,0:T(8,128)(2,1)S(1)} %copy-done.1, f32[1,1024]{1,0:T(1,128)S(1)} %bitcast.10, bf16[1024,3072]{1,0:T(8,128)(2,1)} %w_ref.1, f32[64,1536]{1,0:T(8,128)S(1)} %pad_maximum_fusion.bias_ref, s32[512,1]{1,0:T(8,128)S(1)} %copy.17.gidx_ref, s32[64,8]{1,0:T(8,128)S(1)} %copy.16.cols_ref), custom_call_target="tpu_custom_call" | custom-call | flops 103079215104 | bytes 16777216 | tf_op jit(solution)/shard_map/attend/pallas_call | solution.py:261
  156.1 0.0 copy-done
  156.1 1.3 fusion.29
  157.5 0.0 copy-start.3
  157.5 0.0 copy-start.4
  157.5 1.3 copy-done.3
  158.9 0.3 multiply_reduce_fusion
  159.2 0.0 all-gather.3.cloned.1.call-done
  159.2 19.5 %all-gather.5.cloned.1.call-done = bf16[2048,1024]{1,0:T(8,128)(2,1)} async-done(((bf16[128,1024]{1,0:T(8,128)(2,1)}), bf16[2048,1024]{1,0:T(8,128)(2,1)}) %all-gather.5.cloned.1.call-update) | async-done | bytes 4194320 | tf_op jit(solution)/shard_map/all_gather | solution.py:330
  178.7 0.0 copy-done.4
  178.7 10.3 %add_convert_fusion = bf16[512,1024]{1,0:T(8,128)(2,1)} fusion(f32[512,1024]{1,0:T(8,128)} %copy-done.3, bf16[2048,1024]{1,0:T(8,128)(2,1)} %all-gather.5.cloned.1.call-done, bf16[1024,2048]{1,0:T(8,128)(2,1)} %all-gather.3.cloned.1.call-done, f32[1024]{0:T(1024)S(1)} %copy-done.4, f32[512]{0:T(512)S(1)} %add_rsqrt_fusion, f32[512]{0:T(512)S(1)} %broadcast_multiply_fusion), kind=kOutput, calls=%fused_computation.10 | convolution fusion | flops 4307550208 | bytes 11542528 | tf_op jit(solution)/shard_map/dot_general | solution.py:328
  (2 shorter events, 0.0 us)
Async XLA Ops:
  6.5 149.6 %copy-start = (bf16[1024,1024]{1,0:T(8,128)(2,1)S(1)}, bf16[1024,1024]{1,0:T(8,128)(2,1)}, u32[]{:S(2)}) copy-start(bf16[1024,1024]{1,0:T(8,128)(2,1)} %param.13) | copy-start | bytes 6291460
  6.5 8.3 %copy-start.1 = (bf16[512,1024]{1,0:T(8,128)(2,1)S(1)}, bf16[512,1024]{1,0:T(8,128)(2,1)}, u32[]{:S(2)}) copy-start(bf16[512,1024]{1,0:T(8,128)(2,1)} %x_ref.1) | copy-start | bytes 3145732
  6.5 8.3 %copy-start.2 = (f32[1024]{0:T(1024)S(1)}, f32[1024]{0:T(1024)}, u32[]{:S(2)}) copy-start(f32[1024]{0:T(1024)} %param.11) | copy-start | bytes 12292
  6.5 152.7 %all-gather.3.cloned.1.call-start = ((), (), s32[]{:S(2)}) async-start(), calls=%async_computation | async-start | bytes 4456448 | tf_op jit(solution)/shard_map/all_gather | solution.py:323
  7.3 171.4 %all-gather.5.cloned.1.call-start = ((), (), s32[]{:S(2)}) async-start(), calls=%async_computation.1 | async-start | bytes 4456448 | tf_op jit(solution)/shard_map/all_gather | solution.py:330
  157.5 1.4 copy-start.3
  157.5 21.2 %copy-start.4 = (f32[1024]{0:T(1024)S(1)}, f32[1024]{0:T(1024)}, u32[]{:S(2)}) copy-start(f32[1024]{0:T(1024)} %param.14) | copy-start | bytes 12292
Sparse Core Ops, SparseCore 0:
  9.5 96.6 all-gather.2
  108.4 70.2 all-gather.4

commit v2 on v1

--- a/solution.py
+++ b/solution.py
@@ -310,6 +310,18 @@
         ),
         axis=1,
     ).astype(jnp.float32)
+    groups = lax.axis_size("groups")
+    part = up_weight.shape[1] // groups
+    first = lax.axis_index("groups") * part
+    shard = jnp.concatenate(
+        (
+            lax.dynamic_slice_in_dim(up_weight.T, first, part, 0)[None],
+            lax.dynamic_slice_in_dim(down_weight, first, part, 0)[None],
+        ),
+        axis=0,
+    )
+    gathered = lax.all_gather(shard, ("seq", "groups"), axis=1, tiled=True)
+    up_rows, down_rows = gathered[0], gathered[1]
     attended_rows = attend(
         features, attention_gain, qkv_weight, bias, global_nodes, block_columns
     )
@@ -318,16 +330,17 @@
     )
     normed_mlp = layer_norm(mixed_rows, mlp_gain).astype(jnp.bfloat16)
     hidden = jax.nn.gelu(
-        jnp.dot(
+        lax.dot_general(
             normed_mlp,
-            lax.all_gather(up_weight, "seq", axis=1, tiled=True),
+            up_rows,
+            (((1,), (1,)), ((), ())),
             preferred_element_type=jnp.float32,
         ),
         approximate=True,
     ).astype(jnp.bfloat16)
     reduced = jnp.dot(
         hidden,
-        lax.all_gather(down_weight, "seq", axis=0, tiled=True),
+        down_rows,
         preferred_element_type=jnp.float32,
     )
     return (mixed_rows + reduced).astype(jnp.bfloat16)

time: 196 us -> 179 us (0.913)
  waiting for transfers between devices: 20.9 us -> 0.04 us
  local copies, waits for them, and re-layouts: 3.83 us -> 6.11 us
  Pallas kernels: 141 us -> 143 us
    all_gather x2 -> x1, waiting for transfers between devices: 19.5 us -> 0.02 us  [on_device(): gathered = lax.all_gather(shard, ('seq', 'groups'), axis=1, tiled=True)]
  transfers between devices with their start and end apart: 2 -> 1, of which waited for: 1 -> 0; matrix products, arithmetic and copies ran while one was open for 4% -> 3% of each run, Pallas kernels for 72% -> 80%
where the time goes in v2:
time: 179 us; the launch traced here: 178 us
  Pallas kernels  143 us (80%)
  between operations  13.5 us (8%)
  matrix products  11.7 us (7%)
  local copies, waits for them, and re-layouts  6.11 us (3%)
  other arithmetic  4.25 us (2%)
    pallas_call x1, Pallas kernels, attend(): pl.pallas_call(functools.partial(attention_kernel, n, repeat), out_shape=...  143 us
    dot_general x1, matrix products, on_device(): reduced = jnp.dot(hidden, down_rows, preferred_element_type=jnp.float32)  10.3 us
  transfers between devices with their start and end apart: 1, of which 0 were waited for; matrix products, arithmetic and copies ran while one was open for 3% of the time, Pallas kernels for 80%

profile of v2, /device:TPU:0, one launch (start us, length us, event | category | flops | bytes accessed | tf_op | source)
XLA Modules:
  0.0 178.2 jit_solution(1942694523856268472)
XLA Ops:
  6.5 0.0 copy-start
  6.5 0.0 copy-start.5
  6.5 0.0 copy-start.4
  6.5 0.0 copy-start.1
  6.5 0.0 copy-start.2
  6.5 0.0 all-gather.2.cloned.1.call-start
  6.6 1.7 dynamic-slice_bitcast_fusion
  8.3 1.1 constant_dynamic-slice_fusion
  9.4 0.1 copy.21
  9.6 1.7 pad_maximum_fusion.1
  11.2 0.0 all-gather.2.cloned.1.call-update
  11.2 0.8 copy.17.cols_ref
  12.0 0.7 broadcast_select_fusion.1
  12.7 0.1 broadcast_in_dim.42
  12.9 0.8 copy.24
  13.6 0.0 copy-done.4
  13.6 0.1 copy.18.gidx_ref
  13.8 0.0 copy-done.5
  13.8 0.1 iota_compare_fusion
  13.9 0.4 and_reduce_fusion
  14.3 1.0 pad_maximum_fusion.bias_ref
  15.3 0.0 copy-done.1
  15.3 0.0 copy-done.2
  15.3 142.6 %attend.1 = bf16[512,1024]{1,0:T(8,128)(2,1)S(1)} custom-call(bf16[512,1024]{1,0:T(8,128)(2,1)S(1)} %copy-done.1, f32[1,1024]{1,0:T(1,128)S(1)} %bitcast.27, bf16[1024,3072]{1,0:T(8,128)(2,1)} %w_ref.1, f32[64,1536]{1,0:T(8,128)S(1)} %pad_maximum_fusion.bias_ref, s32[512,1]{1,0:T(8,128)S(1)} %copy.18.gidx_ref, s32[64,8]{1,0:T(8,128)S(1)} %copy.17.cols_ref), custom_call_target="tpu_custom_call" | custom-call | flops 103079215104 | bytes 16777216 | tf_op jit(solution)/shard_map/attend/pallas_call | solution.py:261
  157.9 0.0 copy-done
  157.9 1.4 fusion.22
  159.3 0.0 copy-start.3
  159.3 0.0 copy-start.6
  159.3 1.3 copy-done.3
  160.7 0.3 multiply_reduce_fusion
  161.0 0.0 all-gather.2.cloned.1.call-done
  161.0 0.0 copy-done.6
  161.1 10.3 %add_convert_fusion = bf16[512,1024]{1,0:T(8,128)(2,1)} fusion(f32[512,1024]{1,0:T(8,128)} %copy-done.3, bf16[2,2048,1024]{2,1,0:T(8,128)(2,1)} %all-gather.2.cloned.1.call-done, f32[1024]{0:T(1024)S(1)} %copy-done.6, f32[512]{0:T(512)S(1)} %add_rsqrt_fusion, f32[512]{0:T(512)S(1)} %broadcast_multiply_fusion), kind=kOutput, calls=%fused_computation.13 | convolution fusion | flops 4307550208 | bytes 13639680 | tf_op jit(solution)/shard_map/dot_general | solution.py:341
  (4 shorter events, 0.0 us)
Async XLA Ops:
  6.5 151.4 %copy-start = (bf16[1024,1024]{1,0:T(8,128)(2,1)S(1)}, bf16[1024,1024]{1,0:T(8,128)(2,1)}, u32[]{:S(2)}) copy-start(bf16[1024,1024]{1,0:T(8,128)(2,1)} %param.13) | copy-start | bytes 6291460
  6.5 7.3 %copy-start.5 = (s32[64]{0:T(128)S(1)}, s32[64]{0:T(128)}, u32[]{:S(2)}) copy-start(s32[64]{0:T(128)} %param.18) | copy-start | bytes 772
  6.5 7.1 %copy-start.4 = (s32[512]{0:T(512)S(1)}, s32[512]{0:T(512)}, u32[]{:S(2)}) copy-start(s32[512]{0:T(512)} %param.19) | copy-start | bytes 6148
  6.5 8.8 %copy-start.1 = (bf16[512,1024]{1,0:T(8,128)(2,1)S(1)}, bf16[512,1024]{1,0:T(8,128)(2,1)}, u32[]{:S(2)}) copy-start(bf16[512,1024]{1,0:T(8,128)(2,1)} %x_ref.1) | copy-start | bytes 3145732
  6.5 8.8 %copy-start.2 = (f32[1024]{0:T(1024)S(1)}, f32[1024]{0:T(1024)}, u32[]{:S(2)}) copy-start(f32[1024]{0:T(1024)} %param.11) | copy-start | bytes 12292
  6.5 154.5 %all-gather.2.cloned.1.call-start = ((), (), s32[]{:S(2)}) async-start(), calls=%async_computation | async-start | bytes 8650752 | tf_op jit(solution)/shard_map/all_gather | solution.py:323
  159.3 1.4 copy-start.3
  159.3 1.8 copy-start.6
Sparse Core Ops, SparseCore 0:
  11.4 145.4 all-gather.1

commit v3 on v2

--- a/solution.py
+++ b/solution.py
@@ -35,7 +35,8 @@
     x_ref,
     gain_ref,
     w_ref,
-    bias_ref,
+    used_ref,
+    spots_ref,
     gidx_ref,
     cols_ref,
     out_ref,
@@ -48,6 +49,7 @@
     o_in,
     global_sum,
     global_kv,
+    bias,
     kv_send,
     kv_recv,
     q_send,
@@ -168,6 +170,17 @@
 
     memory[pl.ds(me * blocks, blocks)] = kv_out[my_head]
     q_in[me] = q_out[me]
+
+    used = used_ref[...]
+    global_block = lax.shift_right_logical(spots_ref[...], BLOCK.bit_length() - 1)
+    excluded = jnp.zeros((used.shape[0], global_block.shape[1]), f32)
+    for j in range(slots):
+        listed = used[:, j : j + 1]
+        excluded = jnp.where(listed == global_block, MASKED, excluded)
+        bias[:, j * BLOCK : (j + 1) * BLOCK] = jnp.broadcast_to(
+            jnp.where(listed >= 0, 0.0, MASKED), (used.shape[0], BLOCK)
+        )
+    bias[:, slots * BLOCK :] = excluded
 
     global_sum[...] = jnp.zeros_like(global_sum)
 
@@ -211,7 +224,7 @@
                 (((1,), (1,)), ((), ())),
                 preferred_element_type=f32,
             )
-            weights = jnp.exp(scores + bias_ref[pl.ds(block, 1), :])
+            weights = jnp.exp(scores + bias[pl.ds(block, 1), :])
             totals = jnp.sum(weights, axis=1, keepdims=True)
             scale = jnp.where(totals > 1.0, 2.0**-10, 1.0)
             probs = (weights * (1.0 / (totals * scale))).astype(bf16)
@@ -249,19 +262,20 @@
             out_ref[sub * sub_rows + half : (sub + 1) * sub_rows, at] = bottom.astype(bf16)
 
 
-def attend(features, gain, weight, bias, global_nodes, columns):
+def attend(features, gain, weight, used, global_nodes, columns):
     n = lax.axis_size("seq")
     repeat = n // HEADS
     rows, width = features.shape
     half = rows // repeat // 2
     globals_count = global_nodes.shape[0]
+    keys = columns.shape[1] * BLOCK + globals_count
     bf16 = jnp.bfloat16
     vmem = pl.BlockSpec(memory_space=pltpu.VMEM)
-    flops = 2 * rows * width * 3 * width + 4 * rows * HEADS * 64 * bias.shape[1]
+    flops = 2 * rows * width * 3 * width + 4 * rows * HEADS * 64 * keys
     return pl.pallas_call(
         functools.partial(attention_kernel, n, repeat),
         out_shape=jax.ShapeDtypeStruct((rows, width), bf16),
-        in_specs=[vmem] * 5 + [pl.BlockSpec(memory_space=pltpu.SMEM)],
+        in_specs=[vmem] * 6 + [pl.BlockSpec(memory_space=pltpu.SMEM)],
         out_specs=vmem,
         scratch_shapes=[
             pltpu.VMEM((rows, width), bf16),
@@ -273,16 +287,17 @@
             pltpu.VMEM((n, half, 128), bf16),
             pltpu.VMEM((globals_count, 128), jnp.float32),
             pltpu.VMEM((globals_count, 128), bf16),
+            pltpu.VMEM((columns.shape[0], keys), jnp.float32),
         ]
         + [pltpu.SemaphoreType.DMA((n,))] * 6,
         compiler_params=pltpu.CompilerParams(
             collective_id=0, has_side_effects=True, vmem_limit_bytes=48 * 2**20
         ),
         cost_estimate=pl.CostEstimate(
-            flops=flops * 16, bytes_accessed=2**24, transcendentals=rows * HEADS * bias.shape[1]
+            flops=flops * 16, bytes_accessed=2**24, transcendentals=rows * HEADS * keys
         ),
         name="attend",
-    )(features, gain[None, :], weight, bias, global_nodes[:, None], columns)
+    )(features, gain[None, :], weight, used, global_nodes[None, :], global_nodes[:, None], columns)
 
 
 def on_device(
@@ -299,17 +314,7 @@
 ):
     slots = block_columns.shape[1]
     in_list = jnp.arange(slots, dtype=jnp.int32)[None, :] < block_counts[:, None]
-    global_block = global_nodes // BLOCK
-    duplicate = jnp.any(
-        in_list[:, :, None] & (block_columns[:, :, None] == global_block[None, None, :]), axis=1
-    )
-    bias = jnp.concatenate(
-        (
-            jnp.repeat(jnp.where(in_list, 0.0, MASKED), BLOCK, axis=1),
-            jnp.where(duplicate, MASKED, 0.0),
-        ),
-        axis=1,
-    ).astype(jnp.float32)
+    used = jnp.where(in_list, block_columns, -1)
     groups = lax.axis_size("groups")
     part = up_weight.shape[1] // groups
     first = lax.axis_index("groups") * part
@@ -323,7 +328,7 @@
     gathered = lax.all_gather(shard, ("seq", "groups"), axis=1, tiled=True)
     up_rows, down_rows = gathered[0], gathered[1]
     attended_rows = attend(
-        features, attention_gain, qkv_weight, bias, global_nodes, block_columns
+        features, attention_gain, qkv_weight, used, global_nodes, block_columns
     )
     mixed_rows = features.astype(jnp.float32) + jnp.dot(
         attended_rows, out_weight, preferred_element_type=jnp.float32

time: 179 us -> 178 us (level)
  other arithmetic: 4.25 us -> 2.06 us
  transfers between devices with their start and end apart: 1 -> 1, of which waited for: 0 -> 0; matrix products, arithmetic and copies ran while one was open for 3% -> 2% of each run, Pallas kernels for 80% -> 81%
where the time goes in v3:
time: 178 us; the launch traced here: 177 us
  Pallas kernels  144 us (81%)
  between operations  13.5 us (8%)
  matrix products  11.7 us (7%)
  local copies, waits for them, and re-layouts  5.88 us (3%)
  other arithmetic  2.06 us (1%)
    pallas_call x1, Pallas kernels, attend(): pl.pallas_call(functools.partial(attention_kernel, n, repeat), out_shape=...  144 us
    dot_general x1, matrix products, on_device(): reduced = jnp.dot(hidden, down_rows, preferred_element_type=jnp.float32)  10.4 us
  transfers between devices with their start and end apart: 1, of which 0 were waited for; matrix products, arithmetic and copies ran while one was open for 2% of the time, Pallas kernels for 81%

profile of v3, /device:TPU:0, one launch (start us, length us, event | category | flops | bytes accessed | tf_op | source)
XLA Modules:
  0.0 177.3 jit_solution(672506249855636187)
XLA Ops:
  6.5 0.0 copy-start
  6.5 0.0 copy-start.1
  6.5 0.0 copy-start.5
  6.5 0.0 copy-start.2
  6.5 0.0 copy-start.3
  6.5 0.0 all-gather.2.cloned.1.call-start
  6.6 1.7 dynamic-slice_bitcast_fusion
  8.3 1.1 constant_dynamic-slice_fusion
  9.4 0.1 copy.17
  9.5 1.6 pad_maximum_fusion
  11.2 0.0 all-gather.2.cloned.1.call-update
  11.2 0.8 copy.13.cols_ref
  12.0 0.8 copy.14.gidx_ref
  12.8 0.0 copy-done.5
  12.8 0.1 fusion.16.used_ref
  12.9 0.0 copy-done.1
  12.9 0.0 copy-done.2
  12.9 0.0 copy-done.3
  12.9 144.1 %attend.1 = bf16[512,1024]{1,0:T(8,128)(2,1)S(1)} custom-call(bf16[512,1024]{1,0:T(8,128)(2,1)S(1)} %copy-done.2, f32[1,1024]{1,0:T(1,128)S(1)} %bitcast.26, bf16[1024,3072]{1,0:T(8,128)(2,1)} %w_ref.1, s32[64,8]{1,0:T(8,128)S(1)} %fusion.16.used_ref, s32[1,512]{1,0:T(1,128)S(1)} %bitcast.25, s32[512,1]{1,0:T(8,128)S(1)} %copy.14.gidx_ref, ...), custom_call_target="tpu_custom_call" | custom-call | flops 103079215104 | bytes 16777216 | tf_op jit(solution)/shard_map/attend/pallas_call | solution.py:275
  157.0 0.0 copy-done
  157.0 1.4 fusion.21
  158.4 0.0 copy-start.4
  158.4 0.0 copy-start.6
  158.4 1.3 copy-done.4
  159.7 0.3 multiply_reduce_fusion
  160.1 0.0 all-gather.2.cloned.1.call-done
  160.1 0.0 copy-done.6
  160.1 10.4 %add_convert_fusion = bf16[512,1024]{1,0:T(8,128)(2,1)} fusion(f32[512,1024]{1,0:T(8,128)} %copy-done.4, bf16[2,2048,1024]{2,1,0:T(8,128)(2,1)} %all-gather.2.cloned.1.call-done, f32[1024]{0:T(1024)S(1)} %copy-done.6, f32[512]{0:T(512)S(1)} %add_rsqrt_fusion, f32[512]{0:T(512)S(1)} %broadcast_multiply_fusion), kind=kOutput, calls=%fused_computation.13 | convolution fusion | flops 4307550208 | bytes 13639680 | tf_op jit(solution)/shard_map/dot_general | solution.py:346
  (2 shorter events, 0.0 us)
Async XLA Ops:
  6.5 150.5 %copy-start = (bf16[1024,1024]{1,0:T(8,128)(2,1)S(1)}, bf16[1024,1024]{1,0:T(8,128)(2,1)}, u32[]{:S(2)}) copy-start(bf16[1024,1024]{1,0:T(8,128)(2,1)} %param.13) | copy-start | bytes 6291460
  6.5 6.3 %copy-start.1 = (s32[512]{0:T(512)S(1)}, s32[512]{0:T(512)}, u32[]{:S(2)}) copy-start(s32[512]{0:T(512)} %param.19) | copy-start | bytes 6148
  6.5 6.3 %copy-start.5 = (s32[64]{0:T(128)S(1)}, s32[64]{0:T(128)}, u32[]{:S(2)}) copy-start(s32[64]{0:T(128)} %param.18) | copy-start | bytes 772
  6.5 6.4 %copy-start.2 = (bf16[512,1024]{1,0:T(8,128)(2,1)S(1)}, bf16[512,1024]{1,0:T(8,128)(2,1)}, u32[]{:S(2)}) copy-start(bf16[512,1024]{1,0:T(8,128)(2,1)} %x_ref.1) | copy-start | bytes 3145732
  6.5 6.4 %copy-start.3 = (f32[1024]{0:T(1024)S(1)}, f32[1024]{0:T(1024)}, u32[]{:S(2)}) copy-start(f32[1024]{0:T(1024)} %param.11) | copy-start | bytes 12292
  6.5 153.6 %all-gather.2.cloned.1.call-start = ((), (), s32[]{:S(2)}) async-start(), calls=%async_computation | async-start | bytes 8650752 | tf_op jit(solution)/shard_map/all_gather | solution.py:328
  158.4 1.4 copy-start.4
  158.4 1.7 copy-start.6
Sparse Core Ops, SparseCore 0:
  11.3 143.6 all-gather.1

commit v4 on v3

--- a/solution.py
+++ b/solution.py
@@ -116,7 +116,7 @@
     pl.semaphore_wait(barrier, n - 1)
 
     def quad_of(i):
-        return (me // (4 * repeat) + 1 + i) % (HEADS // 4)
+        return (me // (4 * repeat) + 2 + 3 * i) % (HEADS // 4)
 
     def project(first, quad):
         columns = pl.ds(pl.multiple_of(first * width + quad * 256, 256), 256)
@@ -185,7 +185,7 @@
     global_sum[...] = jnp.zeros_like(global_sum)
 
     def arrive(step, carry):
-        source = (me + n - step) % n
+        source = (me + n // 2 + step) % n
 
         @pl.when(source != me)
         def _():
@@ -202,7 +202,7 @@
     global_kv[...] = global_sum[...].astype(bf16)
 
     def serve(step, carry):
-        source = (me + n - step) % n
+        source = (me + n // 2 + step) % n
 
         @pl.when(source != me)
         def _():

time: 178 us -> 191 us (1.073)
  Pallas kernels: 144 us -> 156 us
    pallas_call x1, Pallas kernels: 144 us -> 156 us  [attend(): pl.pallas_call(functools.partial(attention_kernel, n, repeat), out_shape=...]
  transfers between devices with their start and end apart: 1 -> 1, of which waited for: 0 -> 0; matrix products, arithmetic and copies ran while one was open for 2% -> 2% of each run, Pallas kernels for 81% -> 82%
where the time goes in v4:
time: 191 us; the launch traced here: 189 us
  Pallas kernels  156 us (82%)
  between operations  13.5 us (7%)
  matrix products  11.7 us (6%)
  local copies, waits for them, and re-layouts  5.88 us (3%)
  other arithmetic  2.06 us (1%)
    pallas_call x1, Pallas kernels, attend(): pl.pallas_call(functools.partial(attention_kernel, n, repeat), out_shape=...  156 us
    dot_general x1, matrix products, on_device(): reduced = jnp.dot(hidden, down_rows, preferred_element_type=jnp.float32)  10.4 us
  transfers between devices with their start and end apart: 1, of which 0 were waited for; matrix products, arithmetic and copies ran while one was open for 2% of the time, Pallas kernels for 82%

profile of v4, /device:TPU:0, one launch (start us, length us, event | category | flops | bytes accessed | tf_op | source)
XLA Modules:
  0.0 189.5 jit_solution(13499468615392067919)
XLA Ops:
  6.5 0.0 copy-start
  6.5 0.0 copy-start.1
  6.5 0.0 copy-start.5
  6.5 0.0 copy-start.2
  6.5 0.0 copy-start.3
  6.5 0.0 all-gather.2.cloned.1.call-start
  6.6 1.7 dynamic-slice_bitcast_fusion
  8.3 1.1 constant_dynamic-slice_fusion
  9.4 0.1 copy.17
  9.5 1.6 pad_maximum_fusion
  11.2 0.0 all-gather.2.cloned.1.call-update
  11.2 0.8 copy.13.cols_ref
  12.0 0.8 copy.14.gidx_ref
  12.8 0.0 copy-done.5
  12.8 0.1 fusion.16.used_ref
  12.9 0.0 copy-done.1
  12.9 0.0 copy-done.2
  12.9 0.0 copy-done.3
  12.9 156.2 %attend.1 = bf16[512,1024]{1,0:T(8,128)(2,1)S(1)} custom-call(bf16[512,1024]{1,0:T(8,128)(2,1)S(1)} %copy-done.2, f32[1,1024]{1,0:T(1,128)S(1)} %bitcast.26, bf16[1024,3072]{1,0:T(8,128)(2,1)} %w_ref.1, s32[64,8]{1,0:T(8,128)S(1)} %fusion.16.used_ref, s32[1,512]{1,0:T(1,128)S(1)} %bitcast.25, s32[512,1]{1,0:T(8,128)S(1)} %copy.14.gidx_ref, ...), custom_call_target="tpu_custom_call" | custom-call | flops 103079215104 | bytes 16777216 | tf_op jit(solution)/shard_map/attend/pallas_call | solution.py:275
  169.2 0.0 copy-done
  169.2 1.4 fusion.21
  170.5 0.0 copy-start.4
  170.5 0.0 copy-start.6
  170.6 1.3 copy-done.4
  171.9 0.3 multiply_reduce_fusion
  172.2 0.0 all-gather.2.cloned.1.call-done
  172.3 0.0 copy-done.6
  172.3 10.4 %add_convert_fusion = bf16[512,1024]{1,0:T(8,128)(2,1)} fusion(f32[512,1024]{1,0:T(8,128)} %copy-done.4, bf16[2,2048,1024]{2,1,0:T(8,128)(2,1)} %all-gather.2.cloned.1.call-done, f32[1024]{0:T(1024)S(1)} %copy-done.6, f32[512]{0:T(512)S(1)} %add_rsqrt_fusion, f32[512]{0:T(512)S(1)} %broadcast_multiply_fusion), kind=kOutput, calls=%fused_computation.13 | convolution fusion | flops 4307550208 | bytes 13639680 | tf_op jit(solution)/shard_map/dot_general | solution.py:346
  (2 shorter events, 0.0 us)
Async XLA Ops:
  6.5 162.6 %copy-start = (bf16[1024,1024]{1,0:T(8,128)(2,1)S(1)}, bf16[1024,1024]{1,0:T(8,128)(2,1)}, u32[]{:S(2)}) copy-start(bf16[1024,1024]{1,0:T(8,128)(2,1)} %param.13) | copy-start | bytes 6291460
  6.5 6.3 %copy-start.1 = (s32[512]{0:T(512)S(1)}, s32[512]{0:T(512)}, u32[]{:S(2)}) copy-start(s32[512]{0:T(512)} %param.19) | copy-start | bytes 6148
  6.5 6.3 %copy-start.5 = (s32[64]{0:T(128)S(1)}, s32[64]{0:T(128)}, u32[]{:S(2)}) copy-start(s32[64]{0:T(128)} %param.18) | copy-start | bytes 772
  6.5 6.4 %copy-start.2 = (bf16[512,1024]{1,0:T(8,128)(2,1)S(1)}, bf16[512,1024]{1,0:T(8,128)(2,1)}, u32[]{:S(2)}) copy-start(bf16[512,1024]{1,0:T(8,128)(2,1)} %x_ref.1) | copy-start | bytes 3145732
  6.5 6.4 %copy-start.3 = (f32[1024]{0:T(1024)S(1)}, f32[1024]{0:T(1024)}, u32[]{:S(2)}) copy-start(f32[1024]{0:T(1024)} %param.11) | copy-start | bytes 12292
  6.5 165.7 %all-gather.2.cloned.1.call-start = ((), (), s32[]{:S(2)}) async-start(), calls=%async_computation | async-start | bytes 8650752 | tf_op jit(solution)/shard_map/all_gather | solution.py:328
  170.5 1.4 copy-start.4
  170.5 1.7 copy-start.6
Sparse Core Ops, SparseCore 0:
  11.3 138.0 all-gather.1
